TPU v7x, 32 devices: a whole 2x2x4 slice. The times are simulated.
32 devices in a mesh: dir: 16 (over z, y, x), box: 2 (over core).
Axes of the slice: x: 2, y: 2, z: 4, core: 2. Of those that a mesh axis runs over, the one named last changes fastest.
Arguments:
- child_fields: bfloat16 [256, 8, 2, 512], P(('box', 'dir')), may hold values from -6 to 6
- interp_matrix: bfloat16 [512, 2048], replicated, may hold values from -0.25 to 0.25
- phase_angle: float32 [8, 2048], replicated, may hold values from -3.140625 to 3.140625
- patch_order: int32 [2, 128], P('box'), may hold values from 0 to 127, each once within a row
- offset_code: int32 [16, 16, 40], P('box'), may hold values from 0 to 48
- operator_index: int32 [16, 16, 40], P('box'), may hold values from 0 to 127
- operators: bfloat16 [128, 2, 2048], P(None, None, 'dir'), may hold values from -1 to 1
Outputs:
- local_fields: bfloat16 [256, 8, 2, 512], P(('box', 'dir'))
Inputs may be any that keep to these rules, and one draw needn't show every extreme that they name: `patch_order`: each row holds every number of 0 to 127 once. `offset_code`: entry a names the box offset (a // 7 - 3, a % 7 - 3) on the surface grid, whose two dimensions wrap around.
All inputs are finite; a program needn't handle non-finite values.
Results may differ from a plain program's by a relative error of at most 0.0064.
Values may be sent and summed in bfloat16 or wider, within the bound.
A program may use at most 64 MiB of HBM per device.

v0:
```python
import functools

import jax
import jax.numpy as jnp
from jax import lax
from jax.experimental import pallas as pl
from jax.experimental.pallas import tpu as pltpu
from jax.sharding import PartitionSpec as P

BF = jnp.bfloat16
F32 = jnp.float32
I32 = jnp.int32
REACH = 3
SPAN = 2 * REACH + 1


def onehot(mask):
    return jnp.where(mask, jnp.float32(1), jnp.float32(0))


def mm(a, b):
    return jnp.dot(a, b, preferred_element_type=F32)


def kernel(
    nd, nb, bc, ch, rows, cols,
    child, interp, phase, order, codes, chosen, ops, out,
    order_v, codes_v, chosen_v, ops_v, child_v, interp_v, phase_v, cos_v, sin_v, send_a, recv_a, cnt, weights, gpad,
    halo_out, halo_in, send_b, recv_b,
    load_sem, send_a_sem, recv_a_sem, send_b_sem, recv_b_sem, halo_s_sem, halo_r_sem,
):
    dc, dp = interp.shape
    bw = ops.shape[1]
    nops = ops.shape[0] // 2
    cells = rows * cols
    pair = 2 * bw
    me = lax.axis_index("dir")
    mb = lax.axis_index("box")
    up = lax.rem(mb + 1, nb)
    down = lax.rem(mb + nb - 1, nb)

    loads = [
        pltpu.make_async_copy(child, child_v, load_sem.at[0]),
        pltpu.make_async_copy(phase, phase_v, load_sem.at[1]),
    ]
    for j in range(dp // pair):
        part = pl.ds(j * pair, pair)
        loads.append(
            pltpu.make_async_copy(interp.at[:, part], interp_v.at[:, part], load_sem.at[2 + j])
        )
    tables = [
        pltpu.make_async_copy(source, dest, load_sem.at[len(loads) + i])
        for i, (source, dest) in enumerate(
            ((order, order_v), (codes, codes_v), (chosen, chosen_v), (ops, ops_v)))
    ]
    for copy in loads + tables:
        copy.start()

    far_first = sorted(range(1, nd), key=lambda k: (abs(2 * k - nd), k))
    barrier = pltpu.get_barrier_semaphore()
    for k in far_first:
        pl.semaphore_signal(barrier, inc=1, device_id={"dir": lax.rem(me + k, nd)},
                            device_id_type=pl.DeviceIdType.MESH)
    for other in (up, down):
        pl.semaphore_signal(barrier, inc=1, device_id={"box": other},
                            device_id_type=pl.DeviceIdType.MESH)

    group = 2 * ch
    total = bc * group
    loads[1].wait()
    cos_v[...] = jnp.cos(phase_v[...])
    sin_v[...] = jnp.sin(phase_v[...])
    r0 = lax.broadcasted_iota(I32, (total, total), 0)
    r1 = lax.broadcasted_iota(I32, (total, total), 1)
    bshift = bc.bit_length() - 1
    gshift = group.bit_length() - 1
    pick = onehot(r1 == (r0 & (bc - 1)) * group + (r0 >> bshift)).astype(BF)
    loads[0].wait()
    x = mm(pick, child_v[...].reshape(total, dc)).astype(BF)

    def send_to(target, source, dest, s_sem, r_sem):
        return pltpu.make_async_remote_copy(
            src_ref=source.at[target], dst_ref=dest.at[me], send_sem=s_sem.at[target],
            recv_sem=r_sem.at[me], device_id={"dir": target},
            device_id_type=pl.DeviceIdType.MESH)

    def arrived(source, dest, s_sem, r_sem, slot):
        pltpu.make_async_remote_copy(
            src_ref=source.at[slot], dst_ref=dest.at[slot], send_sem=s_sem.at[slot],
            recv_sem=r_sem.at[slot], device_id={"dir": slot},
            device_id_type=pl.DeviceIdType.MESH).wait_recv()

    for j in range(dp // pair):
        loads[2 + j].wait()
        part = slice(j * pair, (j + 1) * pair)
        prod = mm(x, interp_v[:, part])
        re = jnp.zeros((bc, pair), F32)
        im = jnp.zeros((bc, pair), F32)
        for c in range(ch):
            cc = cos_v[c:c + 1, part]
            ss = sin_v[c:c + 1, part]
            pr = prod[c * 2 * bc:c * 2 * bc + bc]
            pi = prod[c * 2 * bc + bc:(c + 1) * 2 * bc]
            re = re + (cc * pr - ss * pi)
            im = im + (cc * pi + ss * pr)
        block = jnp.concatenate([re, im], axis=0).astype(BF)
        for h in range(2):
            t = 2 * j + h
            send_a[t] = block[:, h * bw:(h + 1) * bw]

    pl.semaphore_wait(barrier, nd + 1)
    for k in far_first:
        send_to(lax.rem(me + k, nd), send_a, recv_a, send_a_sem, recv_a_sem).start()
    recv_a[me] = send_a[me]

    for copy in tables:
        copy.wait()
    q0 = lax.broadcasted_iota(I32, (2 * cells, 2 * cells), 0)
    listed = order_v[...]
    slot = (listed >> bshift) * (2 * bc) + (listed & (bc - 1))
    back = onehot(q0 == jnp.concatenate([slot, slot + bc], axis=1))
    place = jnp.transpose(back).astype(BF)
    back = back.astype(BF)

    o0 = lax.broadcasted_iota(I32, (nops, 2 * nops), 0)
    o1 = lax.broadcasted_iota(I32, (nops, 2 * nops), 1)
    raw = ops_v[...]
    table = jnp.concatenate(
        [mm(onehot(o1 == 2 * o0 + s).astype(BF), raw).astype(BF) for s in range(2)], axis=1)

    half = cells // 2
    nlist = codes.shape[1]
    lanes = ((nlist + 63) // 64) * 64
    fill = jnp.full((half, lanes - nlist), -1, I32)
    code = codes_v[...]
    picked = chosen_v[...]
    both_codes = jnp.concatenate(
        [code[:half], fill, code[half:] + SPAN * SPAN, fill], axis=1)
    both_ops = jnp.concatenate([picked[:half], fill, picked[half:], fill], axis=1)
    span_rows = 2 * SPAN * SPAN
    pad_rows = ((span_rows + 15) // 16) * 16
    m0 = lax.broadcasted_iota(I32, (pad_rows, 2 * lanes), 0)
    n0 = lax.broadcasted_iota(I32, (nops, 2 * lanes), 0)
    for g in range(half):
        left = onehot(m0 == both_codes[g:g + 1]).astype(BF)
        right = onehot(n0 == both_ops[g:g + 1]).astype(BF)
        cnt[g * pad_rows:(g + 1) * pad_rows] = lax.dot_general(
            left, right, (((1,), (1,)), ((), ())), preferred_element_type=F32)
    for f in range(SPAN * SPAN):
        both = jnp.concatenate(
            [cnt[pl.ds(c * SPAN * SPAN + f, half, stride=pad_rows)] for c in range(2)],
            axis=0).astype(BF)
        weight = mm(both, table)
        weights[f, 0] = weight[:, :bw]
        weights[f, 1] = weight[:, bw:]

    for k in range(1, nd):
        arrived(send_a, recv_a, send_a_sem, recv_a_sem, lax.rem(me + k, nd))
    grid = mm(place, recv_a[...].reshape(2 * cells, bw))
    edge = REACH * cols
    for s in range(2):
        halo_out[0, s] = grid[(s + 1) * cells - edge:(s + 1) * cells].astype(BF)
        halo_out[1, s] = grid[s * cells:s * cells + edge].astype(BF)
    halos = [
        pltpu.make_async_remote_copy(
            src_ref=halo_out.at[w], dst_ref=halo_in.at[w], send_sem=halo_s_sem.at[w],
            recv_sem=halo_r_sem.at[w], device_id={"box": other},
            device_id_type=pl.DeviceIdType.MESH)
        for w, other in ((0, up), (1, down))
    ]
    for copy in halos:
        copy.start()

    def lay(s, first, values):
        count = values.shape[0]
        gpad[s, first:first + count, REACH:REACH + cols] = values
        gpad[s, first:first + count, 0:REACH] = values[:, cols - REACH:]
        gpad[s, first:first + count, REACH + cols:2 * REACH + cols] = values[:, :REACH]

    for s in range(2):
        lay(s, REACH, grid[s * cells:(s + 1) * cells].reshape(rows, cols, bw))

    def gather(source_rows, totals):
        totals = list(totals)
        for dv in range(SPAN):
            for r in source_rows:
                sr = gpad[0, r, dv:dv + cols]
                si = gpad[1, r, dv:dv + cols]
                for u in range(rows):
                    du = r - u
                    if 0 <= du < SPAN:
                        f = du * SPAN + dv
                        wr = weights[f, 0, u * cols:(u + 1) * cols]
                        wi = weights[f, 1, u * cols:(u + 1) * cols]
                        tr, ti = totals[u]
                        totals[u] = (tr + (wr * sr - wi * si), ti + (wr * si + wi * sr))
        return totals

    zero = jnp.zeros((cols, bw), F32)
    totals = gather(range(REACH, REACH + rows), [(zero, zero)] * rows)
    for w, first in ((0, 0), (1, REACH + rows)):
        halos[w].wait_recv()
        for s in range(2):
            lay(s, first, halo_in[w, s].astype(F32).reshape(REACH, cols, bw))
    totals = gather(list(range(REACH)) + list(range(REACH + rows, 2 * REACH + rows)), totals)
    moved = jnp.concatenate(
        [totals[u][s] for s in range(2) for u in range(rows)], axis=0).astype(BF)
    send_b[...] = mm(back, moved).astype(BF).reshape(nd, 2 * bc, bw)
    for k in far_first:
        send_to(lax.rem(me + k, nd), send_b, recv_b, send_b_sem, recv_b_sem).start()
    recv_b[me] = send_b[me]

    near_first = [0] + far_first[::-1]
    step = 4 if nd % 4 == 0 else 1
    result = jnp.zeros((total, dc), F32)
    for first in range(0, nd, step):
        blocks, kernels = [], []
        for k in near_first[first:first + step]:
            d = lax.rem(me + k, nd)
            if k:
                arrived(send_b, recv_b, send_b_sem, recv_b_sem, d)
            part = pl.ds(pl.multiple_of(d * bw, bw), bw)
            block = recv_b[d].astype(F32)
            re = block[:bc]
            im = block[bc:]
            pieces = []
            for c in range(ch):
                cc = cos_v[c:c + 1, part]
                ss = sin_v[c:c + 1, part]
                pieces.append(cc * re + ss * im)
                pieces.append(cc * im - ss * re)
            blocks.append(jnp.concatenate(pieces, axis=0).astype(BF))
            kernels.append(interp_v[:, part])
        result = result + lax.dot_general(
            jnp.concatenate(blocks, axis=1), jnp.concatenate(kernels, axis=1),
            (((1,), (1,)), ((), ())), preferred_element_type=F32)
    result = (result * (dc / dp)).astype(BF)
    unpick = onehot(r1 == (r0 & (group - 1)) * bc + (r0 >> gshift)).astype(BF)
    out[...] = mm(unpick, result).astype(BF)

    for k in range(1, nd):
        t = lax.rem(me + k, nd)
        send_to(t, send_a, recv_a, send_a_sem, recv_a_sem).wait_send()
        send_to(t, send_b, recv_b, send_b_sem, recv_b_sem).wait_send()
    for copy in halos:
        copy.wait_send()


def per_device(nd, nb, child, interp, phase, order, codes, chosen, operators):
    bc, ch, _, dc = child.shape
    dp = interp.shape[1]
    rows, cols, nlist = codes.shape
    nops, _, bw = operators.shape
    cells = rows * cols
    lanes = ((nlist + 63) // 64) * 64
    pad_rows = ((2 * SPAN * SPAN + 15) // 16) * 16
    total = bc * ch * 2
    vmem = pl.BlockSpec(memory_space=pltpu.VMEM)
    hbm = pl.BlockSpec(memory_space=pltpu.HBM)
    result = pl.pallas_call(
        functools.partial(kernel, nd, nb, bc, ch, rows, cols),
        out_shape=jax.ShapeDtypeStruct((total, dc), BF),
        in_specs=[hbm] * 7,
        out_specs=vmem,
        scratch_shapes=[
            pltpu.VMEM(order.shape, I32),
            pltpu.VMEM((cells, nlist), I32),
            pltpu.VMEM((cells, nlist), I32),
            pltpu.VMEM((nops * 2, bw), BF),
            pltpu.VMEM((bc * ch, 2, dc), BF),
            pltpu.VMEM((dc, dp), BF),
            pltpu.VMEM((ch, dp), F32),
            pltpu.VMEM((ch, dp), F32),
            pltpu.VMEM((ch, dp), F32),
            pltpu.VMEM((nd, 2 * bc, bw), BF),
            pltpu.VMEM((nd, 2 * bc, bw), BF),
            pltpu.VMEM((cells // 2 * pad_rows, nops), F32),
            pltpu.VMEM((SPAN * SPAN, 2, cells, bw), F32),
            pltpu.VMEM((2, rows + 2 * REACH, 24, bw), F32),
            pltpu.VMEM((2, 2, REACH * cols, bw), BF),
            pltpu.VMEM((2, 2, REACH * cols, bw), BF),
            pltpu.VMEM((nd, 2 * bc, bw), BF),
            pltpu.VMEM((nd, 2 * bc, bw), BF),
            pltpu.SemaphoreType.DMA((6 + dp // (2 * bw),)),
            pltpu.SemaphoreType.DMA((nd,)),
            pltpu.SemaphoreType.DMA((nd,)),
            pltpu.SemaphoreType.DMA((nd,)),
            pltpu.SemaphoreType.DMA((nd,)),
            pltpu.SemaphoreType.DMA((2,)),
            pltpu.SemaphoreType.DMA((2,)),
        ],
        compiler_params=pltpu.CompilerParams(
            collective_id=0, has_side_effects=True, vmem_limit_bytes=24 * 2 ** 20),
    )(*(
        pltpu.with_memory_space_constraint(value, pltpu.HBM)
        for value in (
            child.reshape(bc * ch, 2, dc), interp, phase, order,
            codes.reshape(cells, nlist), chosen.reshape(cells, nlist),
            operators.reshape(nops * 2, bw),
        )
    ))
    return result.reshape(child.shape)


def solution(mesh):
    in_specs = (
        P(("box", "dir"), None, None, None),
        P(),
        P(),
        P("box", None),
        P("box", None, None),
        P("box", None, None),
        P(None, None, "dir"),
    )
    out_specs = P(("box", "dir"), None, None, None)
    return jax.shard_map(
        functools.partial(per_device, mesh.shape["dir"], mesh.shape["box"]),
        mesh=mesh, in_specs=in_specs, out_specs=out_specs, check_vma=False,
    )
```

profile of v0, /device:TPU:0, one launch (start us, length us, event | category | flops | bytes accessed | tf_op | source)
XLA Modules:
  0.0 21.5 jit_solution(8103998605301002159)
XLA Ops:
  0.0 20.8 %shard_map.73 = bf16[128,512]{1,0:T(8,128)(2,1)S(1)} custom-call(bf16[64,2,512]{2,1,0:T(2,128)(2,1)} %bitcast.4, bf16[512,2048]{1,0:T(8,128)(2,1)} %interp.1, f32[8,2048]{1,0:T(8,128)} %phase.1, s32[1,128]{1,0:T(1,128)} %order.1, s32[128,40]{1,0:T(8,128)} %bitcast.5, s32[128,40]{1,0:T(8,128)} %bitcast.6, bf16[256,128]{1,0:T(8,128)(2,1)} %bitcast.7), custom_call_target="tpu_custom_call" | custom-call | tf_op jit(solution)/shard_map/pallas_call | solution.py:260
  20.8 0.7 %reshape.19 = bf16[8,8,2,512]{3,2,1,0:T(2,128)(2,1)} reshape(bf16[128,512]{1,0:T(8,128)(2,1)S(1)} %shard_map.73) | data formatting | bytes 262144 | tf_op jit(solution)/shard_map/reshape | solution.py:302
where the time goes:
time: 21.7 us; the launch traced here: 21.5 us
  Pallas kernels  20.8 us (96%)
  local copies, waits for them, and re-layouts  0.71 us (3%)
    pallas_call x1, Pallas kernels, per_device(): pl.pallas_call(functools.partial(kernel, nd, nb, bc, ch, rows, cols), out...  20.8 us
    reshape x1, local copies, waits for them, and re-layouts, per_device(): return result.reshape(child.shape)  0.71 us

commit v1 on v0

--- a/solution.py
+++ b/solution.py
@@ -22,11 +22,38 @@
     return jnp.dot(a, b, preferred_element_type=F32)
 
 
+SIN = (1.0, -0.16666666541438965, 0.008333329264451874, -0.00019840702862140153,
+       2.751885561882994e-06, -2.3794713199798423e-08)
+COS = (0.4999999954953283, -0.041666640727244325, 0.0013888403499237425,
+       -2.476188584583927e-05, 2.6077099012783433e-07)
+
+
+def horner(coefficients, t):
+    value = jnp.full(t.shape, coefficients[-1], F32)
+    for c in coefficients[-2::-1]:
+        value = value * t + jnp.float32(c)
+    return value
+
+
+def cos_sin(angle):
+    half = angle * 0.5
+    t = half * half
+    sine = half * horner(SIN, t)
+    cosine = 1.0 - t * horner(COS, t)
+    return (cosine - sine) * (cosine + sine), 2.0 * (sine * cosine)
+
+
+def grid_of(nd):
+    across = nd // 2
+    ny = 2 if across % 2 == 0 else 1
+    return across // ny, ny
+
+
 def kernel(
     nd, nb, bc, ch, rows, cols,
     child, interp, phase, order, codes, chosen, ops, out,
     order_v, codes_v, chosen_v, ops_v, child_v, interp_v, phase_v, cos_v, sin_v, send_a, recv_a, cnt, weights, gpad,
-    halo_out, halo_in, send_b, recv_b,
+    halo_out, halo_in, send_b, recv_b, acc_v,
     load_sem, send_a_sem, recv_a_sem, send_b_sem, recv_b_sem, halo_s_sem, halo_r_sem,
 ):
     dc, dp = interp.shape
@@ -34,20 +61,32 @@
     nops = ops.shape[0] // 2
     cells = rows * cols
     pair = 2 * bw
+    nz, ny = grid_of(nd)
+    slots = nz * ny
     me = lax.axis_index("dir")
     mb = lax.axis_index("box")
     up = lax.rem(mb + 1, nb)
     down = lax.rem(mb + nb - 1, nb)
+    mx = lax.rem(me, 2)
+    mq = lax.div(me, 2)
+    my = lax.rem(mq, ny)
+    mz = lax.div(mq, ny)
+
+    def hops(offset):
+        return sum(min(d, n - d) for d, n in zip(offset, (nz, ny)))
+
+    offsets = sorted(((a, b) for a in range(nz) for b in range(ny)),
+                     key=lambda o: (-hops(o), -min(o[0], nz - o[0])))
+    ahead = [lax.rem(mz + a, nz) * ny + lax.rem(my + b, ny) for a, b in offsets]
+    behind = [lax.rem(mz + nz - a, nz) * ny + lax.rem(my + ny - b, ny) for a, b in offsets]
 
     loads = [
         pltpu.make_async_copy(child, child_v, load_sem.at[0]),
         pltpu.make_async_copy(phase, phase_v, load_sem.at[1]),
     ]
-    for j in range(dp // pair):
-        part = pl.ds(j * pair, pair)
-        loads.append(
-            pltpu.make_async_copy(interp.at[:, part], interp_v.at[:, part], load_sem.at[2 + j])
-        )
+    for j in range(slots):
+        part = pl.ds(pl.multiple_of(ahead[j] * pair, pair), pair)
+        loads.append(pltpu.make_async_copy(interp.at[:, part], interp_v.at[j], load_sem.at[2 + j]))
     tables = [
         pltpu.make_async_copy(source, dest, load_sem.at[len(loads) + i])
         for i, (source, dest) in enumerate(
@@ -56,62 +95,80 @@
     for copy in loads + tables:
         copy.start()
 
-    far_first = sorted(range(1, nd), key=lambda k: (abs(2 * k - nd), k))
+    partners = []
+    for j in range(slots):
+        for flip in (1, 0):
+            if j < slots - 1 or flip:
+                partners.append((j, lax.rem(mx + flip, 2), flip))
+
     barrier = pltpu.get_barrier_semaphore()
-    for k in far_first:
-        pl.semaphore_signal(barrier, inc=1, device_id={"dir": lax.rem(me + k, nd)},
+    for j, h, flip in partners:
+        pl.semaphore_signal(barrier, inc=1, device_id={"dir": ahead[j] * 2 + h},
                             device_id_type=pl.DeviceIdType.MESH)
-    for other in (up, down):
+    edges = (up, down) if nb > 2 else (up,)
+    for other in edges:
         pl.semaphore_signal(barrier, inc=1, device_id={"box": other},
                             device_id_type=pl.DeviceIdType.MESH)
 
     group = 2 * ch
     total = bc * group
-    loads[1].wait()
-    cos_v[...] = jnp.cos(phase_v[...])
-    sin_v[...] = jnp.sin(phase_v[...])
     r0 = lax.broadcasted_iota(I32, (total, total), 0)
     r1 = lax.broadcasted_iota(I32, (total, total), 1)
     bshift = bc.bit_length() - 1
-    gshift = group.bit_length() - 1
     pick = onehot(r1 == (r0 & (bc - 1)) * group + (r0 >> bshift)).astype(BF)
     loads[0].wait()
     x = mm(pick, child_v[...].reshape(total, dc)).astype(BF)
-
-    def send_to(target, source, dest, s_sem, r_sem):
-        return pltpu.make_async_remote_copy(
-            src_ref=source.at[target], dst_ref=dest.at[me], send_sem=s_sem.at[target],
-            recv_sem=r_sem.at[me], device_id={"dir": target},
-            device_id_type=pl.DeviceIdType.MESH)
-
-    def arrived(source, dest, s_sem, r_sem, slot):
-        pltpu.make_async_remote_copy(
-            src_ref=source.at[slot], dst_ref=dest.at[slot], send_sem=s_sem.at[slot],
-            recv_sem=r_sem.at[slot], device_id={"dir": slot},
-            device_id_type=pl.DeviceIdType.MESH).wait_recv()
-
-    for j in range(dp // pair):
-        loads[2 + j].wait()
-        part = slice(j * pair, (j + 1) * pair)
-        prod = mm(x, interp_v[:, part])
+    loads[1].wait()
+    for j in range(slots):
+        part = pl.ds(pl.multiple_of(ahead[j] * pair, pair), pair)
+        cos_v[j], sin_v[j] = cos_sin(phase_v[:, part])
+
+    def combine(j, prod):
         re = jnp.zeros((bc, pair), F32)
         im = jnp.zeros((bc, pair), F32)
         for c in range(ch):
-            cc = cos_v[c:c + 1, part]
-            ss = sin_v[c:c + 1, part]
+            cc = cos_v[j, c:c + 1]
+            ss = sin_v[j, c:c + 1]
             pr = prod[c * 2 * bc:c * 2 * bc + bc]
             pi = prod[c * 2 * bc + bc:(c + 1) * 2 * bc]
             re = re + (cc * pr - ss * pi)
             im = im + (cc * pi + ss * pr)
         block = jnp.concatenate([re, im], axis=0).astype(BF)
         for h in range(2):
-            t = 2 * j + h
-            send_a[t] = block[:, h * bw:(h + 1) * bw]
-
-    pl.semaphore_wait(barrier, nd + 1)
-    for k in far_first:
-        send_to(lax.rem(me + k, nd), send_a, recv_a, send_a_sem, recv_a_sem).start()
-    recv_a[me] = send_a[me]
+            send_a[2 * j + h] = block[:, h * bw:(h + 1) * bw]
+
+    def send_first(j, h):
+        return pltpu.make_async_remote_copy(
+            src_ref=send_a.at[2 * j + h], dst_ref=recv_a.at[me], send_sem=send_a_sem,
+            recv_sem=recv_a_sem, device_id={"dir": ahead[j] * 2 + h},
+            device_id_type=pl.DeviceIdType.MESH)
+
+    def send_back(j, h):
+        to = behind[j] * 2 + h
+        return pltpu.make_async_remote_copy(
+            src_ref=send_b.at[to], dst_ref=recv_b.at[2 * j + mx], send_sem=send_b_sem,
+            recv_sem=recv_b_sem.at[j], device_id={"dir": to},
+            device_id_type=pl.DeviceIdType.MESH)
+
+    def whole(source, dest, s_sem, r_sem, first, count):
+        part = pl.ds(first, count)
+        return pltpu.make_async_remote_copy(
+            src_ref=source.at[part], dst_ref=dest.at[part], send_sem=s_sem, recv_sem=r_sem,
+            device_id={"dir": me}, device_id_type=pl.DeviceIdType.MESH)
+
+    last = None
+    for j in range(slots):
+        loads[2 + j].wait()
+        prod = mm(x, interp_v[j])
+        if last is not None:
+            combine(j - 1, last)
+        last = prod
+    combine(slots - 1, last)
+
+    pl.semaphore_wait(barrier, nd - 1 + len(edges))
+    for j, h, flip in partners:
+        send_first(j, h).start()
+    recv_a[me] = send_a[2 * (slots - 1) + mx]
 
     for copy in tables:
         copy.wait()
@@ -154,8 +211,7 @@
         weights[f, 0] = weight[:, :bw]
         weights[f, 1] = weight[:, bw:]
 
-    for k in range(1, nd):
-        arrived(send_a, recv_a, send_a_sem, recv_a_sem, lax.rem(me + k, nd))
+    whole(send_a, recv_a, send_a_sem, recv_a_sem, 0, nd - 1).wait_recv()
     grid = mm(place, recv_a[...].reshape(2 * cells, bw))
     edge = REACH * cols
     for s in range(2):
@@ -206,44 +262,36 @@
     moved = jnp.concatenate(
         [totals[u][s] for s in range(2) for u in range(rows)], axis=0).astype(BF)
     send_b[...] = mm(back, moved).astype(BF).reshape(nd, 2 * bc, bw)
-    for k in far_first:
-        send_to(lax.rem(me + k, nd), send_b, recv_b, send_b_sem, recv_b_sem).start()
-    recv_b[me] = send_b[me]
-
-    near_first = [0] + far_first[::-1]
-    step = 4 if nd % 4 == 0 else 1
-    result = jnp.zeros((total, dc), F32)
-    for first in range(0, nd, step):
-        blocks, kernels = [], []
-        for k in near_first[first:first + step]:
-            d = lax.rem(me + k, nd)
-            if k:
-                arrived(send_b, recv_b, send_b_sem, recv_b_sem, d)
-            part = pl.ds(pl.multiple_of(d * bw, bw), bw)
-            block = recv_b[d].astype(F32)
-            re = block[:bc]
-            im = block[bc:]
-            pieces = []
-            for c in range(ch):
-                cc = cos_v[c:c + 1, part]
-                ss = sin_v[c:c + 1, part]
-                pieces.append(cc * re + ss * im)
-                pieces.append(cc * im - ss * re)
-            blocks.append(jnp.concatenate(pieces, axis=0).astype(BF))
-            kernels.append(interp_v[:, part])
-        result = result + lax.dot_general(
-            jnp.concatenate(blocks, axis=1), jnp.concatenate(kernels, axis=1),
-            (((1,), (1,)), ((), ())), preferred_element_type=F32)
-    result = (result * (dc / dp)).astype(BF)
-    unpick = onehot(r1 == (r0 & (group - 1)) * bc + (r0 >> gshift)).astype(BF)
-    out[...] = mm(unpick, result).astype(BF)
-
-    for k in range(1, nd):
-        t = lax.rem(me + k, nd)
-        send_to(t, send_a, recv_a, send_a_sem, recv_a_sem).wait_send()
-        send_to(t, send_b, recv_b, send_b_sem, recv_b_sem).wait_send()
+    for j, h, flip in partners:
+        send_back(j, h).start()
+    recv_b[2 * (slots - 1) + mx] = send_b[me]
+    whole(send_a, recv_a, send_a_sem, recv_a_sem, 0, nd - 1).wait_send()
     for copy in halos:
         copy.wait_send()
+
+    def shifted(j):
+        block = jnp.concatenate([recv_b[2 * j], recv_b[2 * j + 1]], axis=1).astype(F32)
+        re = block[:bc]
+        im = block[bc:]
+        pieces = []
+        for c in range(ch):
+            cc = cos_v[j, c:c + 1]
+            ss = sin_v[j, c:c + 1]
+            pieces.append(cc * re + ss * im)
+            pieces.append(cc * im - ss * re)
+        return jnp.concatenate(pieces, axis=0).astype(BF)
+
+    near_first = list(range(slots))[::-1]
+    for i, j in enumerate(near_first):
+        if i == slots - 1:
+            whole(send_b, recv_b, send_b_sem, recv_b_sem.at[j], 0, nd - 1).wait_send()
+        whole(send_b, recv_b, send_b_sem, recv_b_sem.at[j], 2 * j, 1 if i == 0 else 2).wait_recv()
+        term = lax.dot_general(
+            shifted(j), interp_v[j], (((1,), (1,)), ((), ())), preferred_element_type=F32)
+        if i < slots - 1:
+            acc_v[...] = term if i == 0 else acc_v[...] + term
+        else:
+            out[...] = ((acc_v[...] + term) * (dc / dp)).astype(BF)
 
 
 def per_device(nd, nb, child, interp, phase, order, codes, chosen, operators):
@@ -252,6 +300,8 @@
     rows, cols, nlist = codes.shape
     nops, _, bw = operators.shape
     cells = rows * cols
+    nz, ny = grid_of(nd)
+    slots = nz * ny
     lanes = ((nlist + 63) // 64) * 64
     pad_rows = ((2 * SPAN * SPAN + 15) // 16) * 16
     total = bc * ch * 2
@@ -268,10 +318,10 @@
             pltpu.VMEM((cells, nlist), I32),
             pltpu.VMEM((nops * 2, bw), BF),
             pltpu.VMEM((bc * ch, 2, dc), BF),
-            pltpu.VMEM((dc, dp), BF),
+            pltpu.VMEM((slots, dc, 2 * bw), BF),
             pltpu.VMEM((ch, dp), F32),
-            pltpu.VMEM((ch, dp), F32),
-            pltpu.VMEM((ch, dp), F32),
+            pltpu.VMEM((slots, ch, 2 * bw), F32),
+            pltpu.VMEM((slots, ch, 2 * bw), F32),
             pltpu.VMEM((nd, 2 * bc, bw), BF),
             pltpu.VMEM((nd, 2 * bc, bw), BF),
             pltpu.VMEM((cells // 2 * pad_rows, nops), F32),
@@ -281,11 +331,12 @@
             pltpu.VMEM((2, 2, REACH * cols, bw), BF),
             pltpu.VMEM((nd, 2 * bc, bw), BF),
             pltpu.VMEM((nd, 2 * bc, bw), BF),
-            pltpu.SemaphoreType.DMA((6 + dp // (2 * bw),)),
-            pltpu.SemaphoreType.DMA((nd,)),
-            pltpu.SemaphoreType.DMA((nd,)),
-            pltpu.SemaphoreType.DMA((nd,)),
-            pltpu.SemaphoreType.DMA((nd,)),
+            pltpu.VMEM((total, dc), F32),
+            pltpu.SemaphoreType.DMA((6 + slots,)),
+            pltpu.SemaphoreType.DMA,
+            pltpu.SemaphoreType.DMA,
+            pltpu.SemaphoreType.DMA,
+            pltpu.SemaphoreType.DMA((slots,)),
             pltpu.SemaphoreType.DMA((2,)),
             pltpu.SemaphoreType.DMA((2,)),
         ],
@@ -299,7 +350,7 @@
             operators.reshape(nops * 2, bw),
         )
     ))
-    return result.reshape(child.shape)
+    return result.reshape(ch, 2, bc, dc).transpose(2, 0, 1, 3)
 
 
 def solution(mesh):

time: 21.7 us -> 19.6 us (0.903)
  Pallas kernels: 20.8 us -> 18.7 us
    pallas_call x1, Pallas kernels: 20.8 us -> 18.7 us  [per_device(): pl.pallas_call(functools.partial(kernel, nd, nb, bc, ch, rows, cols), out...]
where the time goes in v1:
time: 19.6 us; the launch traced here: 19.5 us
  Pallas kernels  18.7 us (95%)
  local copies, waits for them, and re-layouts  0.76 us (4%)
    pallas_call x1, Pallas kernels, per_device(): pl.pallas_call(functools.partial(kernel, nd, nb, bc, ch, rows, cols), out...  18.7 us
    reshape x1, local copies, waits for them, and re-layouts, per_device(): return result.reshape(ch, 2, bc, dc).transpose(2, 0, 1, 3)  0.76 us

profile of v1, /device:TPU:0, one launch (start us, length us, event | category | flops | bytes accessed | tf_op | source)
XLA Modules:
  0.0 19.5 jit_solution(11912523751968109232)
XLA Ops:
  0.0 18.7 %shard_map.73 = bf16[128,512]{1,0:T(8,128)(2,1)S(1)} custom-call(bf16[64,2,512]{2,1,0:T(2,128)(2,1)} %bitcast.9, bf16[512,2048]{1,0:T(8,128)(2,1)} %interp.1, f32[8,2048]{1,0:T(8,128)} %phase.1, s32[1,128]{1,0:T(1,128)} %order.1, s32[128,40]{1,0:T(8,128)} %bitcast.10, s32[128,40]{1,0:T(8,128)} %bitcast.11, bf16[256,128]{1,0:T(8,128)(2,1)} %bitcast.12), custom_call_target="tpu_custom_call" | custom-call | tf_op jit(solution)/shard_map/pallas_call | solution.py:310
  18.7 0.8 %copy.10 = bf16[8,2,8,512]{3,1,0,2:T(2,128)(2,1)} copy(bf16[8,2,8,512]{3,2,1,0:T(8,128)(2,1)S(1)} %bitcast.8) | data formatting | bytes 262144 | tf_op jit(solution)/shard_map/reshape | solution.py:353

commit v2 on v1

--- a/solution.py
+++ b/solution.py
@@ -53,8 +53,8 @@
     nd, nb, bc, ch, rows, cols,
     child, interp, phase, order, codes, chosen, ops, out,
     order_v, codes_v, chosen_v, ops_v, child_v, interp_v, phase_v, cos_v, sin_v, send_a, recv_a, cnt, weights, gpad,
-    halo_out, halo_in, send_b, recv_b, acc_v,
-    load_sem, send_a_sem, recv_a_sem, send_b_sem, recv_b_sem, halo_s_sem, halo_r_sem,
+    halo_out, halo_in, send_b, recv_b, acc_v, interp_t,
+    slot_sem, recv_a_sem, halo_s_sem, halo_r_sem, child_sem, phase_sem, order_sem, codes_sem, ops_sem,
 ):
     dc, dp = interp.shape
     bw = ops.shape[1]
@@ -75,30 +75,22 @@
     def hops(offset):
         return sum(min(d, n - d) for d, n in zip(offset, (nz, ny)))
 
-    offsets = sorted(((a, b) for a in range(nz) for b in range(ny)),
-                     key=lambda o: (-hops(o), -min(o[0], nz - o[0])))
+    offsets = [(a, b) for a in range(nz) for b in range(ny)]
+    far = sorted(range(slots), key=lambda j: (-hops(offsets[j]), -min(offsets[j][0], nz - offsets[j][0])))
+
+    def slot_of(a, b):
+        return a * ny + b
+
+    def reach(d):
+        return d // 2 // ny + d // 2 % ny + d % 2
+
     ahead = [lax.rem(mz + a, nz) * ny + lax.rem(my + b, ny) for a, b in offsets]
     behind = [lax.rem(mz + nz - a, nz) * ny + lax.rem(my + ny - b, ny) for a, b in offsets]
 
-    loads = [
-        pltpu.make_async_copy(child, child_v, load_sem.at[0]),
-        pltpu.make_async_copy(phase, phase_v, load_sem.at[1]),
-    ]
-    for j in range(slots):
-        part = pl.ds(pl.multiple_of(ahead[j] * pair, pair), pair)
-        loads.append(pltpu.make_async_copy(interp.at[:, part], interp_v.at[j], load_sem.at[2 + j]))
-    tables = [
-        pltpu.make_async_copy(source, dest, load_sem.at[len(loads) + i])
-        for i, (source, dest) in enumerate(
-            ((order, order_v), (codes, codes_v), (chosen, chosen_v), (ops, ops_v)))
-    ]
-    for copy in loads + tables:
-        copy.start()
-
     partners = []
-    for j in range(slots):
+    for j in far:
         for flip in (1, 0):
-            if j < slots - 1 or flip:
+            if j or flip:
                 partners.append((j, lax.rem(mx + flip, 2), flip))
 
     barrier = pltpu.get_barrier_semaphore()
@@ -110,15 +102,31 @@
         pl.semaphore_signal(barrier, inc=1, device_id={"box": other},
                             device_id_type=pl.DeviceIdType.MESH)
 
+    first_loads = [
+        pltpu.make_async_copy(child, child_v, child_sem),
+        pltpu.make_async_copy(phase, phase_v, phase_sem),
+    ]
+    columns = []
+    for i, j in enumerate(far):
+        part = pl.ds(pl.multiple_of(ahead[j] * pair, pair), pair)
+        columns.append(pltpu.make_async_copy(interp.at[:, part], interp_v.at[j], slot_sem.at[i]))
+    tables = [
+        pltpu.make_async_copy(source, dest, sem)
+        for source, dest, sem in (
+            (order, order_v, order_sem), (codes, codes_v, codes_sem), (chosen, chosen_v, halo_s_sem), (ops, ops_v, ops_sem))
+    ]
+    for copy in first_loads + columns + tables:
+        copy.start()
+
     group = 2 * ch
     total = bc * group
     r0 = lax.broadcasted_iota(I32, (total, total), 0)
     r1 = lax.broadcasted_iota(I32, (total, total), 1)
     bshift = bc.bit_length() - 1
     pick = onehot(r1 == (r0 & (bc - 1)) * group + (r0 >> bshift)).astype(BF)
-    loads[0].wait()
+    first_loads[0].wait()
     x = mm(pick, child_v[...].reshape(total, dc)).astype(BF)
-    loads[1].wait()
+    first_loads[1].wait()
     for j in range(slots):
         part = pl.ds(pl.multiple_of(ahead[j] * pair, pair), pair)
         cos_v[j], sin_v[j] = cos_sin(phase_v[:, part])
@@ -139,15 +147,15 @@
 
     def send_first(j, h):
         return pltpu.make_async_remote_copy(
-            src_ref=send_a.at[2 * j + h], dst_ref=recv_a.at[me], send_sem=send_a_sem,
+            src_ref=send_a.at[2 * j + h], dst_ref=recv_a.at[me], send_sem=child_sem,
             recv_sem=recv_a_sem, device_id={"dir": ahead[j] * 2 + h},
             device_id_type=pl.DeviceIdType.MESH)
 
     def send_back(j, h):
         to = behind[j] * 2 + h
         return pltpu.make_async_remote_copy(
-            src_ref=send_b.at[to], dst_ref=recv_b.at[2 * j + mx], send_sem=send_b_sem,
-            recv_sem=recv_b_sem.at[j], device_id={"dir": to},
+            src_ref=send_b.at[to], dst_ref=recv_b.at[2 * j + mx], send_sem=phase_sem,
+            recv_sem=slot_sem.at[j], device_id={"dir": to},
             device_id_type=pl.DeviceIdType.MESH)
 
     def whole(source, dest, s_sem, r_sem, first, count):
@@ -157,21 +165,29 @@
             device_id={"dir": me}, device_id_type=pl.DeviceIdType.MESH)
 
     last = None
-    for j in range(slots):
-        loads[2 + j].wait()
+    for i, j in enumerate(far):
+        columns[i].wait()
         prod = mm(x, interp_v[j])
         if last is not None:
-            combine(j - 1, last)
+            combine(far[i - 1], last)
         last = prod
-    combine(slots - 1, last)
+    combine(0, last)
 
     pl.semaphore_wait(barrier, nd - 1 + len(edges))
-    for j, h, flip in partners:
-        send_first(j, h).start()
-    recv_a[me] = send_a[2 * (slots - 1) + mx]
+    for to in sorted(range(nd), key=lambda d: (-reach(d), -d)):
+        @pl.when(me != to)
+        def _():
+            a, b = to // 2 // ny, to // 2 % ny
+            place = slot_of(lax.rem(a + nz - mz, nz), lax.rem(b + ny - my, ny))
+            pltpu.make_async_remote_copy(
+                src_ref=send_a.at[2 * place + to % 2], dst_ref=recv_a.at[me], send_sem=child_sem,
+                recv_sem=recv_a_sem, device_id={"dir": to},
+                device_id_type=pl.DeviceIdType.MESH).start()
+    recv_a[me] = send_a[mx]
 
     for copy in tables:
         copy.wait()
+
     q0 = lax.broadcasted_iota(I32, (2 * cells, 2 * cells), 0)
     listed = order_v[...]
     slot = (listed >> bshift) * (2 * bc) + (listed & (bc - 1))
@@ -208,10 +224,12 @@
             [cnt[pl.ds(c * SPAN * SPAN + f, half, stride=pad_rows)] for c in range(2)],
             axis=0).astype(BF)
         weight = mm(both, table)
-        weights[f, 0] = weight[:, :bw]
-        weights[f, 1] = weight[:, bw:]
-
-    whole(send_a, recv_a, send_a_sem, recv_a_sem, 0, nd - 1).wait_recv()
+        wr, wi = weight[:, :bw], weight[:, bw:]
+        weights[f, 0] = wr
+        weights[f, 1] = wr + wi
+        weights[f, 2] = wi - wr
+
+    whole(send_a, recv_a, child_sem, recv_a_sem, 0, nd - 1).wait_recv()
     grid = mm(place, recv_a[...].reshape(2 * cells, bw))
     edge = REACH * cols
     for s in range(2):
@@ -219,55 +237,66 @@
         halo_out[1, s] = grid[s * cells:s * cells + edge].astype(BF)
     halos = [
         pltpu.make_async_remote_copy(
-            src_ref=halo_out.at[w], dst_ref=halo_in.at[w], send_sem=halo_s_sem.at[w],
-            recv_sem=halo_r_sem.at[w], device_id={"box": other},
+            src_ref=halo_out.at[w], dst_ref=halo_in.at[w], send_sem=halo_s_sem,
+            recv_sem=halo_r_sem, device_id={"box": other},
             device_id_type=pl.DeviceIdType.MESH)
         for w, other in ((0, up), (1, down))
     ]
     for copy in halos:
         copy.start()
 
-    def lay(s, first, values):
-        count = values.shape[0]
-        gpad[s, first:first + count, REACH:REACH + cols] = values
-        gpad[s, first:first + count, 0:REACH] = values[:, cols - REACH:]
-        gpad[s, first:first + count, REACH + cols:2 * REACH + cols] = values[:, :REACH]
-
-    for s in range(2):
-        lay(s, REACH, grid[s * cells:(s + 1) * cells].reshape(rows, cols, bw))
-
+    def lay(first, re, im):
+        count = re.shape[0]
+        for s, values in enumerate((re + im, im, re)):
+            gpad[s, first:first + count, REACH:REACH + cols] = values
+            gpad[s, first:first + count, 0:REACH] = values[:, cols - REACH:]
+            gpad[s, first:first + count, REACH + cols:2 * REACH + cols] = values[:, :REACH]
+
+    lay(REACH, *(grid[s * cells:(s + 1) * cells].reshape(rows, cols, bw) for s in range(2)))
+
+    tile = 8
     def gather(source_rows, totals):
-        totals = list(totals)
-        for dv in range(SPAN):
-            for r in source_rows:
-                sr = gpad[0, r, dv:dv + cols]
-                si = gpad[1, r, dv:dv + cols]
-                for u in range(rows):
-                    du = r - u
-                    if 0 <= du < SPAN:
-                        f = du * SPAN + dv
-                        wr = weights[f, 0, u * cols:(u + 1) * cols]
-                        wi = weights[f, 1, u * cols:(u + 1) * cols]
-                        tr, ti = totals[u]
-                        totals[u] = (tr + (wr * sr - wi * si), ti + (wr * si + wi * sr))
+        totals = dict(totals)
+        for v in range(0, cols, tile):
+            for dv in range(SPAN):
+                for r in source_rows:
+                    source = [gpad[s, r, v + dv:v + dv + tile] for s in range(3)]
+                    for u in range(rows):
+                        du = r - u
+                        if 0 <= du < SPAN:
+                            f = du * SPAN + dv
+                            at = slice(u * cols + v, u * cols + v + tile)
+                            totals[u, v] = [
+                                t + weights[f, s, at] * source[s] for s, t in enumerate(totals[u, v])]
         return totals
 
-    zero = jnp.zeros((cols, bw), F32)
-    totals = gather(range(REACH, REACH + rows), [(zero, zero)] * rows)
+    zero = jnp.zeros((tile, bw), F32)
+    totals = {(u, v): [zero] * 3 for u in range(rows) for v in range(0, cols, tile)}
+    totals = gather(range(REACH, REACH + rows), totals)
+    both_halos = pltpu.make_async_remote_copy(
+        src_ref=halo_out, dst_ref=halo_in, send_sem=halo_s_sem, recv_sem=halo_r_sem,
+        device_id={"box": mb}, device_id_type=pl.DeviceIdType.MESH)
+    both_halos.wait_recv()
     for w, first in ((0, 0), (1, REACH + rows)):
-        halos[w].wait_recv()
-        for s in range(2):
-            lay(s, first, halo_in[w, s].astype(F32).reshape(REACH, cols, bw))
+        lay(first, *(halo_in[w, s].astype(F32).reshape(REACH, cols, bw) for s in range(2)))
     totals = gather(list(range(REACH)) + list(range(REACH + rows, 2 * REACH + rows)), totals)
-    moved = jnp.concatenate(
-        [totals[u][s] for s in range(2) for u in range(rows)], axis=0).astype(BF)
+    moved = jnp.concatenate([k[0] - k[1] for k in totals.values()] + [k[0] + k[2] for k in totals.values()], axis=0).astype(BF)
     send_b[...] = mm(back, moved).astype(BF).reshape(nd, 2 * bc, bw)
-    for j, h, flip in partners:
-        send_back(j, h).start()
-    recv_b[2 * (slots - 1) + mx] = send_b[me]
-    whole(send_a, recv_a, send_a_sem, recv_a_sem, 0, nd - 1).wait_send()
-    for copy in halos:
-        copy.wait_send()
+    for to in sorted(range(nd), key=lambda d: (reach(d), d)):
+        @pl.when(me != to)
+        def _():
+            a, b = to // 2 // ny, to // 2 % ny
+            place = slot_of(lax.rem(mz + nz - a, nz), lax.rem(my + ny - b, ny))
+            pltpu.make_async_remote_copy(
+                src_ref=send_b.at[to], dst_ref=recv_b.at[2 * place + mx], send_sem=phase_sem,
+                recv_sem=slot_sem.at[place], device_id={"dir": to},
+                device_id_type=pl.DeviceIdType.MESH).start()
+    recv_b[mx] = send_b[me]
+    whole(send_a, recv_a, child_sem, recv_a_sem, 0, nd - 1).wait_send()
+    both_halos.wait_send()
+
+    for j in range(slots):
+        interp_t[j] = jnp.transpose(interp_v[j])
 
     def shifted(j):
         block = jnp.concatenate([recv_b[2 * j], recv_b[2 * j + 1]], axis=1).astype(F32)
@@ -281,13 +310,12 @@
             pieces.append(cc * im - ss * re)
         return jnp.concatenate(pieces, axis=0).astype(BF)
 
-    near_first = list(range(slots))[::-1]
+    near_first = far[::-1]
     for i, j in enumerate(near_first):
         if i == slots - 1:
-            whole(send_b, recv_b, send_b_sem, recv_b_sem.at[j], 0, nd - 1).wait_send()
-        whole(send_b, recv_b, send_b_sem, recv_b_sem.at[j], 2 * j, 1 if i == 0 else 2).wait_recv()
-        term = lax.dot_general(
-            shifted(j), interp_v[j], (((1,), (1,)), ((), ())), preferred_element_type=F32)
+            whole(send_b, recv_b, phase_sem, slot_sem.at[j], 0, nd - 1).wait_send()
+        whole(send_b, recv_b, phase_sem, slot_sem.at[j], 2 * j, 1 if i == 0 else 2).wait_recv()
+        term = mm(shifted(j), interp_t[j])
         if i < slots - 1:
             acc_v[...] = term if i == 0 else acc_v[...] + term
         else:
@@ -325,23 +353,26 @@
             pltpu.VMEM((nd, 2 * bc, bw), BF),
             pltpu.VMEM((nd, 2 * bc, bw), BF),
             pltpu.VMEM((cells // 2 * pad_rows, nops), F32),
-            pltpu.VMEM((SPAN * SPAN, 2, cells, bw), F32),
-            pltpu.VMEM((2, rows + 2 * REACH, 24, bw), F32),
+            pltpu.VMEM((SPAN * SPAN, 3, cells, bw), F32),
+            pltpu.VMEM((3, rows + 2 * REACH, 24, bw), F32),
             pltpu.VMEM((2, 2, REACH * cols, bw), BF),
             pltpu.VMEM((2, 2, REACH * cols, bw), BF),
             pltpu.VMEM((nd, 2 * bc, bw), BF),
             pltpu.VMEM((nd, 2 * bc, bw), BF),
             pltpu.VMEM((total, dc), F32),
-            pltpu.SemaphoreType.DMA((6 + slots,)),
-            pltpu.SemaphoreType.DMA,
-            pltpu.SemaphoreType.DMA,
-            pltpu.SemaphoreType.DMA,
+            pltpu.VMEM((slots, 2 * bw, dc), BF),
             pltpu.SemaphoreType.DMA((slots,)),
-            pltpu.SemaphoreType.DMA((2,)),
-            pltpu.SemaphoreType.DMA((2,)),
+            pltpu.SemaphoreType.DMA,
+            pltpu.SemaphoreType.DMA,
+            pltpu.SemaphoreType.DMA,
+            pltpu.SemaphoreType.DMA,
+            pltpu.SemaphoreType.DMA,
+            pltpu.SemaphoreType.DMA,
+            pltpu.SemaphoreType.DMA,
+            pltpu.SemaphoreType.DMA,
         ],
         compiler_params=pltpu.CompilerParams(
-            collective_id=0, has_side_effects=True, vmem_limit_bytes=24 * 2 ** 20),
+            collective_id=0, has_side_effects=True, vmem_limit_bytes=32 * 2 ** 20),
     )(*(
         pltpu.with_memory_space_constraint(value, pltpu.HBM)
         for value in (

time: 19.6 us -> 18.5 us (0.944)
  Pallas kernels: 18.7 us -> 17.6 us
    pallas_call x1, Pallas kernels: 18.7 us -> 17.6 us  [per_device(): pl.pallas_call(functools.partial(kernel, nd, nb, bc, ch, rows, cols), out...]
where the time goes in v2:
time: 18.5 us; the launch traced here: 18.3 us
  Pallas kernels  17.6 us (95%)
  local copies, waits for them, and re-layouts  0.76 us (4%)
    pallas_call x1, Pallas kernels, per_device(): pl.pallas_call(functools.partial(kernel, nd, nb, bc, ch, rows, cols), out...  17.6 us
    reshape x1, local copies, waits for them, and re-layouts, per_device(): return result.reshape(ch, 2, bc, dc).transpose(2, 0, 1, 3)  0.76 us

profile of v2, /device:TPU:0, one launch (start us, length us, event | category | flops | bytes accessed | tf_op | source)
XLA Modules:
  0.0 18.3 jit_solution(15477432889944012186)
XLA Ops:
  0.0 17.6 %shard_map.73 = bf16[128,512]{1,0:T(8,128)(2,1)S(1)} custom-call(bf16[64,2,512]{2,1,0:T(2,128)(2,1)} %bitcast.9, bf16[512,2048]{1,0:T(8,128)(2,1)} %interp.1, f32[8,2048]{1,0:T(8,128)} %phase.1, s32[1,128]{1,0:T(1,128)} %order.1, s32[128,40]{1,0:T(8,128)} %bitcast.10, s32[128,40]{1,0:T(8,128)} %bitcast.11, bf16[256,128]{1,0:T(8,128)(2,1)} %bitcast.12), custom_call_target="tpu_custom_call" | custom-call | tf_op jit(solution)/shard_map/pallas_call | solution.py:338
  17.6 0.8 %copy.10 = bf16[8,2,8,512]{3,1,0,2:T(2,128)(2,1)} copy(bf16[8,2,8,512]{3,2,1,0:T(8,128)(2,1)S(1)} %bitcast.8) | data formatting | bytes 262144 | tf_op jit(solution)/shard_map/reshape | solution.py:384

commit v3 on v2

--- a/solution.py
+++ b/solution.py
@@ -53,7 +53,7 @@
     nd, nb, bc, ch, rows, cols,
     child, interp, phase, order, codes, chosen, ops, out,
     order_v, codes_v, chosen_v, ops_v, child_v, interp_v, phase_v, cos_v, sin_v, send_a, recv_a, cnt, weights, gpad,
-    halo_out, halo_in, send_b, recv_b, acc_v, interp_t,
+    halo_out, halo_in, send_b, recv_b, acc_v, interp_t, first_w, first_in, first_halo, send_first_b,
     slot_sem, recv_a_sem, halo_s_sem, halo_r_sem, child_sem, phase_sem, order_sem, codes_sem, ops_sem,
 ):
     dc, dp = interp.shape
@@ -229,9 +229,59 @@
         weights[f, 1] = wr + wi
         weights[f, 2] = wi - wr
 
+    edge = REACH * cols
+    spans = SPAN * SPAN
+    entries = spans + spans % 2
+
+    def prepare_first():
+        cshift = cols.bit_length() - 1
+        held = onehot(listed == lax.broadcasted_iota(I32, (bc, cells), 0))
+        cell = lax.broadcasted_iota(I32, (bc, cells), 1)
+        home_u = jnp.sum(held * (cell >> cshift).astype(F32), axis=1, keepdims=True).astype(I32)
+        home_v = jnp.sum(held * (cell & (cols - 1)).astype(F32), axis=1, keepdims=True).astype(I32)
+        held = held.astype(BF)
+        none = jnp.full((bc, lanes - nlist), -1, I32)
+        own_code = jnp.concatenate([mm(held, code.astype(F32).astype(BF)).astype(I32), none], axis=1)
+        own_ops = jnp.concatenate([mm(held, picked.astype(F32).astype(BF)).astype(I32), none], axis=1)
+        box_rows = ((spans + 15) // 16) * 16
+        m1 = lax.broadcasted_iota(I32, (box_rows, lanes), 0)
+        n1 = lax.broadcasted_iota(I32, (nops, lanes), 0)
+        for g in range(bc):
+            left = onehot(m1 == own_code[g:g + 1]).astype(BF)
+            right = onehot(n1 == own_ops[g:g + 1]).astype(BF)
+            cnt[g * box_rows:(g + 1) * box_rows] = lax.dot_general(
+                left, right, (((1,), (1,)), ((), ())), preferred_element_type=F32)
+        times = [cnt[pl.ds(f, bc, stride=box_rows)] for f in range(spans)]
+        times += [jnp.zeros((bc, nops), F32)] * (entries - spans)
+        weight = mm(jnp.concatenate(times, axis=0).astype(BF), table)
+        wr, wi = weight[:, :bw], weight[:, bw:]
+        first_w[0] = wr
+        first_w[1] = wr + wi
+        first_w[2] = wi - wr
+
+        lane = lax.broadcasted_iota(I32, (bc, cells), 1)
+        halo_lane = lax.broadcasted_iota(I32, (bc, 4 * edge), 1)
+        wide_u = jnp.broadcast_to(home_u, (bc, 4 * edge))
+        wide_v = jnp.broadcast_to(home_v, (bc, 4 * edge))
+        inside, beyond = [], [[], []]
+        for f in range(entries):
+            r = wide_u + (f // SPAN - REACH)
+            at = r * cols + ((wide_v + (f % SPAN - REACH)) & (cols - 1))
+            inside.append(onehot(at[:, :cells] == lane))
+            past = jnp.where(r < 0, at + edge, jnp.where(r >= rows, at - cells + 2 * edge, -4 * edge))
+            for s in range(2):
+                beyond[s].append(onehot(past + s * edge == halo_lane))
+        inside = jnp.concatenate(inside, axis=0).astype(BF)
+        for s in range(2):
+            part = slice(s * entries * bc, (s + 1) * entries * bc)
+            first_in[part] = mm(inside, place[s * cells:(s + 1) * cells]).astype(BF)
+            first_halo[part] = jnp.concatenate(beyond[s], axis=0).astype(BF)
+
+    late_core = lax.rem(mb, 2)
+    pl.when(late_core == 0)(prepare_first)
+
     whole(send_a, recv_a, child_sem, recv_a_sem, 0, nd - 1).wait_recv()
     grid = mm(place, recv_a[...].reshape(2 * cells, bw))
-    edge = REACH * cols
     for s in range(2):
         halo_out[0, s] = grid[(s + 1) * cells - edge:(s + 1) * cells].astype(BF)
         halo_out[1, s] = grid[s * cells:s * cells + edge].astype(BF)
@@ -244,6 +294,27 @@
     ]
     for copy in halos:
         copy.start()
+    pl.when(late_core != 0)(prepare_first)
+    both_halos = pltpu.make_async_remote_copy(
+        src_ref=halo_out, dst_ref=halo_in, send_sem=halo_s_sem, recv_sem=halo_r_sem,
+        device_id={"box": mb}, device_id_type=pl.DeviceIdType.MESH)
+
+    @pl.when(me != 0)
+    def _():
+        both_halos.wait_recv()
+        found = mm(first_in[...], recv_a[...].reshape(2 * cells, bw)) + mm(
+            first_halo[...], halo_in[...].reshape(4 * edge, bw))
+        sums = [jnp.zeros((bc, bw), F32)] * 3
+        for f in range(spans):
+            re = found[f * bc:(f + 1) * bc]
+            im = found[(entries + f) * bc:(entries + f + 1) * bc]
+            sums = [t + first_w[s, f * bc:(f + 1) * bc] * z for s, (t, z) in enumerate(zip(sums, (re + im, im, re)))]
+        send_first_b[...] = jnp.concatenate([sums[0] - sums[1], sums[0] + sums[2]], axis=0).astype(BF)
+        slot = slot_of(mz, my)
+        pltpu.make_async_remote_copy(
+            src_ref=send_first_b, dst_ref=recv_b.at[2 * slot + mx], send_sem=phase_sem,
+            recv_sem=slot_sem.at[slot], device_id={"dir": 0},
+            device_id_type=pl.DeviceIdType.MESH).start()
 
     def lay(first, re, im):
         count = re.shape[0]
@@ -273,16 +344,17 @@
     zero = jnp.zeros((tile, bw), F32)
     totals = {(u, v): [zero] * 3 for u in range(rows) for v in range(0, cols, tile)}
     totals = gather(range(REACH, REACH + rows), totals)
-    both_halos = pltpu.make_async_remote_copy(
-        src_ref=halo_out, dst_ref=halo_in, send_sem=halo_s_sem, recv_sem=halo_r_sem,
-        device_id={"box": mb}, device_id_type=pl.DeviceIdType.MESH)
-    both_halos.wait_recv()
+
+    @pl.when(me == 0)
+    def _():
+        both_halos.wait_recv()
+
     for w, first in ((0, 0), (1, REACH + rows)):
         lay(first, *(halo_in[w, s].astype(F32).reshape(REACH, cols, bw) for s in range(2)))
     totals = gather(list(range(REACH)) + list(range(REACH + rows, 2 * REACH + rows)), totals)
     moved = jnp.concatenate([k[0] - k[1] for k in totals.values()] + [k[0] + k[2] for k in totals.values()], axis=0).astype(BF)
     send_b[...] = mm(back, moved).astype(BF).reshape(nd, 2 * bc, bw)
-    for to in sorted(range(nd), key=lambda d: (reach(d), d)):
+    for to in sorted(range(1, nd), key=lambda d: (reach(d), d)):
         @pl.when(me != to)
         def _():
             a, b = to // 2 // ny, to // 2 % ny
@@ -330,6 +402,7 @@
     cells = rows * cols
     nz, ny = grid_of(nd)
     slots = nz * ny
+    entries = SPAN * SPAN + SPAN * SPAN % 2
     lanes = ((nlist + 63) // 64) * 64
     pad_rows = ((2 * SPAN * SPAN + 15) // 16) * 16
     total = bc * ch * 2
@@ -361,6 +434,10 @@
             pltpu.VMEM((nd, 2 * bc, bw), BF),
             pltpu.VMEM((total, dc), F32),
             pltpu.VMEM((slots, 2 * bw, dc), BF),
+            pltpu.VMEM((3, entries * bc, bw), F32),
+            pltpu.VMEM((2 * entries * bc, 2 * cells), BF),
+            pltpu.VMEM((2 * entries * bc, 4 * REACH * cols), BF),
+            pltpu.VMEM((2 * bc, bw), BF),
             pltpu.SemaphoreType.DMA((slots,)),
             pltpu.SemaphoreType.DMA,
             pltpu.SemaphoreType.DMA,

time: 18.5 us -> 18 us (0.973)
  Pallas kernels: 17.6 us -> 17.1 us
    pallas_call x1, Pallas kernels: 17.6 us -> 17.1 us  [per_device(): pl.pallas_call(functools.partial(kernel, nd, nb, bc, ch, rows, cols), out...]
where the time goes in v3:
time: 18 us; the launch traced here: 17.9 us
  Pallas kernels  17.1 us (95%)
  local copies, waits for them, and re-layouts  0.76 us (4%)
    pallas_call x1, Pallas kernels, per_device(): pl.pallas_call(functools.partial(kernel, nd, nb, bc, ch, rows, cols), out...  17.1 us
    reshape x1, local copies, waits for them, and re-layouts, per_device(): return result.reshape(ch, 2, bc, dc).transpose(2, 0, 1, 3)  0.76 us

profile of v3, /device:TPU:0, one launch (start us, length us, event | category | flops | bytes accessed | tf_op | source)
XLA Modules:
  0.0 17.9 jit_solution(5549048176657040956)
XLA Ops:
  0.0 17.1 %shard_map.73 = bf16[128,512]{1,0:T(8,128)(2,1)S(1)} custom-call(bf16[64,2,512]{2,1,0:T(2,128)(2,1)} %bitcast.9, bf16[512,2048]{1,0:T(8,128)(2,1)} %interp.1, f32[8,2048]{1,0:T(8,128)} %phase.1, s32[1,128]{1,0:T(1,128)} %order.1, s32[128,40]{1,0:T(8,128)} %bitcast.10, s32[128,40]{1,0:T(8,128)} %bitcast.11, bf16[256,128]{1,0:T(8,128)(2,1)} %bitcast.12), custom_call_target="tpu_custom_call" | custom-call | tf_op jit(solution)/shard_map/pallas_call | solution.py:411
  17.1 0.8 %copy.10 = bf16[8,2,8,512]{3,1,0,2:T(2,128)(2,1)} copy(bf16[8,2,8,512]{3,2,1,0:T(8,128)(2,1)S(1)} %bitcast.8) | data formatting | bytes 262144 | tf_op jit(solution)/shard_map/reshape | solution.py:461

commit v4 on v3

--- a/solution.py
+++ b/solution.py
@@ -53,7 +53,7 @@
     nd, nb, bc, ch, rows, cols,
     child, interp, phase, order, codes, chosen, ops, out,
     order_v, codes_v, chosen_v, ops_v, child_v, interp_v, phase_v, cos_v, sin_v, send_a, recv_a, cnt, weights, gpad,
-    halo_out, halo_in, send_b, recv_b, acc_v, interp_t, first_w, first_in, first_halo, send_first_b,
+    halo_out, halo_in, send_b, recv_b, acc_v, interp_t, first_w, first_in, send_first_b,
     slot_sem, recv_a_sem, halo_s_sem, halo_r_sem, child_sem, phase_sem, order_sem, codes_sem, ops_sem,
 ):
     dc, dp = interp.shape
@@ -274,8 +274,8 @@
         inside = jnp.concatenate(inside, axis=0).astype(BF)
         for s in range(2):
             part = slice(s * entries * bc, (s + 1) * entries * bc)
-            first_in[part] = mm(inside, place[s * cells:(s + 1) * cells]).astype(BF)
-            first_halo[part] = jnp.concatenate(beyond[s], axis=0).astype(BF)
+            first_in[part, :2 * cells] = mm(inside, place[s * cells:(s + 1) * cells]).astype(BF)
+            first_in[part, 2 * cells:] = jnp.concatenate(beyond[s], axis=0).astype(BF)
 
     late_core = lax.rem(mb, 2)
     pl.when(late_core == 0)(prepare_first)
@@ -302,8 +302,8 @@
     @pl.when(me != 0)
     def _():
         both_halos.wait_recv()
-        found = mm(first_in[...], recv_a[...].reshape(2 * cells, bw)) + mm(
-            first_halo[...], halo_in[...].reshape(4 * edge, bw))
+        found = mm(first_in[...], jnp.concatenate(
+            [recv_a[...].reshape(2 * cells, bw), halo_in[...].reshape(4 * edge, bw)], axis=0))
         sums = [jnp.zeros((bc, bw), F32)] * 3
         for f in range(spans):
             re = found[f * bc:(f + 1) * bc]
@@ -384,14 +384,13 @@
 
     near_first = far[::-1]
     for i, j in enumerate(near_first):
-        if i == slots - 1:
-            whole(send_b, recv_b, phase_sem, slot_sem.at[j], 0, nd - 1).wait_send()
         whole(send_b, recv_b, phase_sem, slot_sem.at[j], 2 * j, 1 if i == 0 else 2).wait_recv()
         term = mm(shifted(j), interp_t[j])
         if i < slots - 1:
             acc_v[...] = term if i == 0 else acc_v[...] + term
         else:
             out[...] = ((acc_v[...] + term) * (dc / dp)).astype(BF)
+    whole(send_b, recv_b, phase_sem, slot_sem.at[0], 0, nd - 1).wait_send()
 
 
 def per_device(nd, nb, child, interp, phase, order, codes, chosen, operators):
@@ -435,8 +434,7 @@
             pltpu.VMEM((total, dc), F32),
             pltpu.VMEM((slots, 2 * bw, dc), BF),
             pltpu.VMEM((3, entries * bc, bw), F32),
-            pltpu.VMEM((2 * entries * bc, 2 * cells), BF),
-            pltpu.VMEM((2 * entries * bc, 4 * REACH * cols), BF),
+            pltpu.VMEM((2 * entries * bc, 2 * cells + 4 * REACH * cols), BF),
             pltpu.VMEM((2 * bc, bw), BF),
             pltpu.SemaphoreType.DMA((slots,)),
             pltpu.SemaphoreType.DMA,

time: 18 us -> 18 us (level)
  no operation moved by 1% of the time
where the time goes in v4:
time: 18 us; the launch traced here: 17.8 us
  Pallas kernels  17.1 us (95%)
  local copies, waits for them, and re-layouts  0.76 us (4%)
    pallas_call x1, Pallas kernels, per_device(): pl.pallas_call(functools.partial(kernel, nd, nb, bc, ch, rows, cols), out...  17.1 us
    reshape x1, local copies, waits for them, and re-layouts, per_device(): return result.reshape(ch, 2, bc, dc).transpose(2, 0, 1, 3)  0.76 us

profile of v4, /device:TPU:0, one launch (start us, length us, event | category | flops | bytes accessed | tf_op | source)
XLA Modules:
  0.0 17.8 jit_solution(6949354569483748714)
XLA Ops:
  0.0 17.1 %shard_map.73 = bf16[128,512]{1,0:T(8,128)(2,1)S(1)} custom-call(bf16[64,2,512]{2,1,0:T(2,128)(2,1)} %bitcast.9, bf16[512,2048]{1,0:T(8,128)(2,1)} %interp.1, f32[8,2048]{1,0:T(8,128)} %phase.1, s32[1,128]{1,0:T(1,128)} %order.1, s32[128,40]{1,0:T(8,128)} %bitcast.10, s32[128,40]{1,0:T(8,128)} %bitcast.11, bf16[256,128]{1,0:T(8,128)(2,1)} %bitcast.12), custom_call_target="tpu_custom_call" | custom-call | tf_op jit(solution)/shard_map/pallas_call | solution.py:410
  17.1 0.8 %copy.10 = bf16[8,2,8,512]{3,1,0,2:T(2,128)(2,1)} copy(bf16[8,2,8,512]{3,2,1,0:T(8,128)(2,1)S(1)} %bitcast.8) | data formatting | bytes 262144 | tf_op jit(solution)/shard_map/reshape | solution.py:459
